TPU v7x, 256 devices: a whole 4x4x8 slice. The times are simulated.
256 devices in a mesh: lat: 4 (over z_lo), wave: 64 (over z_hi, y, x, core).
Axes of the slice: x: 4, y: 4, z: 8 (z_hi: 2, z_lo: 4; z = z_hi * 4 + z_lo), core: 2. Of those that a mesh axis runs over, the one named last changes fastest.
Arguments:
- fourier: bfloat16 [2, 1024, 1024, 128], P(None, ('lat', 'wave')), may hold values from -6 to 6
- cycle_points: int32 [1024], P(('lat', 'wave')), may hold values from 20 to 4120, as said below
- wave_table: int32 [1024], replicated, may hold values from 0 to 1023, as said below
- legendre: bfloat16 [1024, 1024, 1024], P('wave', 'lat'), as said below
Outputs:
- spectral: bfloat16 [1024, 1024, 128], P('wave', 'lat')
Inputs may be any that keep to these rules, and one draw needn't show every extreme that they name: wave_table is a permutation of 0 to 1023; slots 16 q to 16 q + 15 hold 16 consecutive wavenumbers in rising order. legendre[r, k, l] is zero wherever the degree wave_table[r] + 2 j + p exceeds 1024 - 1, with p = 1 if l >= 512 else 0 and j = l - p * 512. `cycle_points`: cycle k has about 4 k + 20 points.
All inputs are finite; a program needn't handle non-finite values.
Results may differ from a plain program's by a relative error of at most 0.0085.
Values may be sent and summed in bfloat16 or wider, within the bound.
No kernel may reach another device: no remote copies, remote signals or barrier semaphores. Data moves between devices by JAX's collectives and lax.ppermute only.
A program may use at most 128 MiB of HBM per device.

v0:
```python
import jax
import jax.numpy as jnp
from jax import lax
from jax.sharding import PartitionSpec as P


def contract(piece, inputs, bands):
    slots, cycles, columns = piece.shape
    cycle_band = cycles // bands
    left = piece.reshape(slots, bands, cycle_band, columns)
    right = inputs.reshape(bands, cycle_band, inputs.shape[1], inputs.shape[2])
    parts = jnp.einsum("mbkl,bkmc->bmlc", left, right, preferred_element_type=jnp.float32)
    return jnp.sum(parts.astype(jnp.bfloat16).astype(jnp.float32), axis=0)


def project(legendre, inputs, bands):
    return contract(legendre, inputs, bands)


def per_device(fourier, cycle_points, wave_table, legendre):
    waves_all = wave_table.shape[0]
    half = waves_all // 2
    waves = jnp.arange(waves_all, dtype=jnp.int32)
    present = (2 * waves[None, :] < cycle_points[:, None]).astype(jnp.bfloat16)
    kept = fourier * present[None, :, :, None]
    ordered = jnp.take(kept, wave_table, axis=2)
    banded = lax.all_to_all(ordered, "wave", split_axis=2, concat_axis=1, tiled=True)
    north = banded[0].astype(jnp.float32)
    south = banded[1].astype(jnp.float32)
    even_part = (north + south).astype(jnp.bfloat16)
    odd_part = (north - south).astype(jnp.bfloat16)
    moved = lax.all_to_all(legendre, "lat", split_axis=2, concat_axis=1, tiled=True)
    block_cols = moved.shape[2]
    first_col = lax.axis_index("lat") * block_cols
    parity = (first_col >= half).astype(jnp.int32)
    even_all, odd_all = (
        lax.all_gather(even_part, "lat", axis=0, tiled=True),
        lax.all_gather(odd_part, "lat", axis=0, tiled=True),
    )
    gathered = jnp.where(parity == 1, odd_all, even_all)
    result = project(moved, gathered, lax.axis_size("lat"))
    return result.astype(jnp.bfloat16)


def solution(mesh):
    placed = (P(None, ("lat", "wave"), None, None), P(("lat", "wave")), P(), P("wave", "lat", None))
    return jax.shard_map(
        per_device, mesh=mesh, in_specs=placed, out_specs=P("wave", "lat", None), check_vma=False
    )
```

profile of v0, /device:TPU:1, one launch (start us, length us, event | category | flops | bytes accessed | tf_op | source)
XLA Modules:
  0.0 455.1 jit_solution(8741149732136601205)
XLA Ops:
  6.5 0.0 all-gather.3.cloned.1.call-start
  6.5 0.7 fusion.9
  7.2 0.7 compare_and_fusion
  7.9 0.7 compare_convert_fusion
  8.7 0.2 copy.17
  8.9 4.6 %copy_multiply_fusion = bf16[2,4,1024,128]{3,1,2,0:T(4,128)(2,1)} fusion(bf16[2,4,1024,128]{3,2,1,0:T(8,128)(2,1)} %param.4, bf16[4,1024]{0,1:T(8,128)(2,1)S(1)} %copy.17), kind=kLoop, calls=%fused_computation.11 | loop fusion | flops 1048576 | bytes 4202496 | tf_op jit(solution)/shard_map/mul | solution.py:25
  13.4 6.0 %gather_fusion = bf16[1024,2,4,128]{3,2,1,0:T(4,128)(2,1)S(1)} fusion(bf16[2,4,1024,128]{3,1,2,0:T(4,128)(2,1)} %copy_multiply_fusion, s32[1024]{0:T(1024)S(1)} %fusion.9), kind=kCustom, calls=%fused_computation | custom fusion | bytes 4198400 | tf_op jit(solution)/shard_map/jit(_take)/gather | solution.py:26
  19.5 3.8 select_bitcast_fusion
  23.3 53.2 %all_to_all.30 = bf16[2,4,1024,128]{3,1,0,2:T(4,128)(2,1)S(1)} all-to-all(bf16[2,4,1024,128]{3,1,0,2:T(4,128)(2,1)S(1)} %select_bitcast_fusion), channel_id=1, replica_groups=mesh['lat'=4,'wave'=64] {'wave'}, dimensions={2} | all-to-all | bytes 4194304 | tf_op jit(solution)/shard_map/all_to_all | solution.py:27
  76.5 0.6 copy.33
  77.2 1.9 fusion.8
  79.1 0.0 all-gather.3.cloned.1.call-update
  79.1 12.6 %copy.20 = bf16[16,256,1024]{1,0,2:T(8,128)(2,1)} copy(bf16[16,256,1024]{2,1,0:T(8,128)(2,1)} %param.7) | data formatting | bytes 16777216 | tf_op args[3]
  91.7 18.9 %all-to-all-start.1 = ((bf16[16,256,1024]{1,0,2:T(8,128)(2,1)}), bf16[16,256,1024]{1,0,2:T(8,128)(2,1)}, u32[]{:S(2)}, u32[]{:S(2)}) async-start(bf16[16,256,1024]{1,0,2:T(8,128)(2,1)} %copy.20), calls=%async_computation.1 | async-start | bytes 16777216 | tf_op jit(solution)/shard_map/all_to_all | solution.py:32
  110.6 0.0 all-gather.5.cloned.1.call-start
  110.6 0.7 all-gather.5.cloned.1.call-update
  111.3 136.6 %all-gather.3.cloned.1.call-done = bf16[1024,16,128]{2,1,0:T(8,128)(2,1)} async-done(((bf16[256,16,128]{2,1,0:T(8,128)(2,1)}), bf16[1024,16,128]{2,1,0:T(8,128)(2,1)}) %all-gather.3.cloned.1.call-update) | async-done | bytes 4194320 | tf_op jit(solution)/shard_map/all_gather | solution.py:38
  247.9 174.3 %all-gather.5.cloned.1.call-done = bf16[1024,16,128]{2,1,0:T(8,128)(2,1)} async-done(((bf16[256,16,128]{2,1,0:T(8,128)(2,1)}), bf16[1024,16,128]{2,1,0:T(8,128)(2,1)}) %all-gather.5.cloned.1.call-update) | async-done | bytes 4194320 | tf_op jit(solution)/shard_map/all_gather | solution.py:37
  422.2 4.6 %broadcast_select_fusion = bf16[1024,16,128]{2,1,0:T(8,128)(2,1)} fusion(bf16[1024,16,128]{2,1,0:T(8,128)(2,1)} %all-gather.3.cloned.1.call-done, bf16[1024,16,128]{2,1,0:T(8,128)(2,1)} %all-gather.5.cloned.1.call-done, pred[]{:T(512)S(6)} %eq.3), kind=kLoop, calls=%fused_computation.5 | loop fusion | flops 2097152 | bytes 12582913 | tf_op jit(solution)/shard_map/jit(_where)/select_n | solution.py:40
  426.8 0.0 all-to-all-done.1
  426.8 13.8 %copy.22 = bf16[16,256,4,256]{3,1,0,2:T(8,128)(2,1)} copy(bf16[16,256,4,256]{1,0,3,2:T(8,128)(2,1)} %bitcast.6) | data formatting | bytes 16777216 | tf_op jit(solution)/shard_map/all_to_all | solution.py:32
  440.6 6.3 %convert_reduce_fusion = bf16[16,128,256]{2,1,0:T(8,128)(2,1)S(1)} fusion(bf16[16,256,4,256]{3,1,0,2:T(8,128)(2,1)} %copy.22, bf16[4,256,16,128]{3,2,1,0:T(8,128)(2,1)} %bitcast.18), kind=kOutput, calls=%fused_computation.4 | convolution fusion | flops 1077411840 | bytes 13631488 | tf_op jit(solution)/shard_map/mbkl,bkmc->bmlc/dot_general | solution.py:12
  446.9 1.3 copy.24
  (1 shorter events, 0.0 us)
Async XLA Ops:
  6.5 241.4 %all-gather.3.cloned.1.call-start = ((), (), s32[]{:S(2)}) async-start(), calls=%async_computation.2 | async-start | bytes 5242880 | tf_op jit(solution)/shard_map/all_gather | solution.py:38
  91.7 335.1 %all-to-all-start.1 = ((bf16[16,256,1024]{1,0,2:T(8,128)(2,1)}), bf16[16,256,1024]{1,0,2:T(8,128)(2,1)}, u32[]{:S(2)}, u32[]{:S(2)}) async-start(bf16[16,256,1024]{1,0,2:T(8,128)(2,1)} %copy.20), calls=%async_computation.1 | async-start | bytes 16777216 | tf_op jit(solution)/shard_map/all_to_all | solution.py:32
  110.6 311.6 %all-gather.5.cloned.1.call-start = ((), (), s32[]{:S(2)}) async-start(), calls=%async_computation.3 | async-start | bytes 5242880 | tf_op jit(solution)/shard_map/all_gather | solution.py:37
Sparse Core Ops, SparseCore 0:
  79.2 168.6 all-gather.2
  249.7 172.4 all-gather.4
where the time goes:
time: 456 us; the launch traced here: 455 us
  waiting for transfers between devices  312 us (68%)
  blocking collectives  53.2 us (12%)
  local copies, waits for them, and re-layouts  34.6 us (8%)
  starting transfers between devices  18.9 us (4%)
  other arithmetic  17 us (4%)
  between operations  13.4 us (3%)
  matrix products  6.34 us (1%)
    all_gather x1, waiting for transfers between devices, per_device(): lax.all_gather(even_part, 'lat', axis=0, tiled=True)  174 us
    all_gather x1, waiting for transfers between devices, per_device(): lax.all_gather(odd_part, 'lat', axis=0, tiled=True)  137 us
    all_to_all x1, blocking collectives, per_device(): lax.all_to_all(ordered, 'wave', split_axis=2, concat_axis=1, tiled=True)  53.2 us
    all_to_all x1, starting transfers between devices, per_device(): lax.all_to_all(legendre, 'lat', split_axis=2, concat_axis=1, tiled=True)  18.9 us
    all_to_all x1, local copies, waits for them, and re-layouts, per_device(): lax.all_to_all(legendre, 'lat', split_axis=2, concat_axis=1, tiled=True)  13.8 us
    unnamed x1, local copies, waits for them, and re-layouts  12.6 us
  transfers between devices with their start and end apart: 3, of which 2 were waited for; matrix products, arithmetic and copies ran while one was open for 4% of the time, Pallas kernels for 0%

commit v1 on v0

--- a/solution.py
+++ b/solution.py
@@ -2,6 +2,13 @@
 import jax.numpy as jnp
 from jax import lax
 from jax.sharding import PartitionSpec as P
+
+
+def find_teams(w_in, peer_axis, d_out):
+    oldest = jnp.concatenate(
+        lax.all_to_all(jnp.stack([w_in] * lax.axis_size(peer_axis)), peer_axis, 0, 0), axis=d_out
+    )
+    return oldest
 
 
 def contract(piece, inputs, bands):
@@ -34,7 +41,7 @@
     first_col = lax.axis_index("lat") * block_cols
     parity = (first_col >= half).astype(jnp.int32)
     even_all, odd_all = (
-        lax.all_gather(even_part, "lat", axis=0, tiled=True),
+        find_teams(even_part, "lat", 0),
         lax.all_gather(odd_part, "lat", axis=0, tiled=True),
     )
     gathered = jnp.where(parity == 1, odd_all, even_all)

time: 456 us -> 479 us (1.050)
  waiting for transfers between devices: 312 us -> 328 us
  starting transfers between devices: 18.9 us -> 24.3 us
    all_gather x1 -> x0, waiting for transfers between devices: 174 us -> none  [per_device(): lax.all_gather(even_part, 'lat', axis=0, tiled=True)]
    all_to_all x1, waiting for transfers between devices: 0.01 us -> 94.3 us  [per_device(): lax.all_to_all(legendre, 'lat', split_axis=2, concat_axis=1, tiled=True)]
    all_to_all x0 -> x1, waiting for transfers between devices: none -> 82.1 us  [find_teams(): lax.all_to_all(jnp.stack([w_in] * lax.axis_size(peer_axis)), peer_axis, 0...]
    all_to_all x0 -> x1, starting transfers between devices: none -> 18.6 us  [find_teams(): lax.all_to_all(jnp.stack([w_in] * lax.axis_size(peer_axis)), peer_axis, 0...]
    all_gather x1, waiting for transfers between devices: 137 us -> 151 us  [per_device(): lax.all_gather(odd_part, 'lat', axis=0, tiled=True)]
    all_to_all x1, starting transfers between devices: 18.9 us -> 5.64 us  [per_device(): lax.all_to_all(legendre, 'lat', split_axis=2, concat_axis=1, tiled=True)]
  transfers between devices with their start and end apart: 3 -> 3, of which waited for: 2 -> 3; matrix products, arithmetic and copies ran while one was open for 4% -> 4% of each run, Pallas kernels for 0% -> 0%
where the time goes in v1:
time: 479 us; the launch traced here: 478 us
  waiting for transfers between devices  328 us (68%)
  blocking collectives  53.2 us (11%)
  local copies, waits for them, and re-layouts  37 us (8%)
  starting transfers between devices  24.3 us (5%)
  other arithmetic  16.5 us (3%)
  between operations  13.5 us (3%)
  matrix products  6.34 us (1%)
    all_gather x1, waiting for transfers between devices, per_device(): lax.all_gather(odd_part, 'lat', axis=0, tiled=True)  151 us
    all_to_all x1, waiting for transfers between devices, per_device(): lax.all_to_all(legendre, 'lat', split_axis=2, concat_axis=1, tiled=True)  94.3 us
    all_to_all x1, waiting for transfers between devices, find_teams(): lax.all_to_all(jnp.stack([w_in] * lax.axis_size(peer_axis)), peer_axis, 0...  82.1 us
    all_to_all x1, blocking collectives, per_device(): lax.all_to_all(ordered, 'wave', split_axis=2, concat_axis=1, tiled=True)  53.2 us
    all_to_all x1, starting transfers between devices, find_teams(): lax.all_to_all(jnp.stack([w_in] * lax.axis_size(peer_axis)), peer_axis, 0...  18.6 us
    all_to_all x1, local copies, waits for them, and re-layouts, per_device(): lax.all_to_all(legendre, 'lat', split_axis=2, concat_axis=1, tiled=True)  13.7 us
    unnamed x1, local copies, waits for them, and re-layouts  12.6 us
  transfers between devices with their start and end apart: 3, of which 3 were waited for; matrix products, arithmetic and copies ran while one was open for 4% of the time, Pallas kernels for 0%

profile of v1, /device:TPU:1, one launch (start us, length us, event | category | flops | bytes accessed | tf_op | source)
XLA Modules:
  0.0 478.4 jit_solution(2572070027382079758)
XLA Ops:
  6.5 0.7 compare_and_fusion
  7.2 0.7 fusion.9
  7.9 0.7 compare_convert_fusion
  8.7 0.2 copy.17
  8.9 4.6 copy_multiply_fusion
  13.4 6.0 %gather_fusion = bf16[1024,2,4,128]{3,2,1,0:T(4,128)(2,1)S(1)} fusion(bf16[2,4,1024,128]{3,1,2,0:T(4,128)(2,1)} %copy_multiply_fusion, s32[1024]{0:T(1024)S(1)} %fusion.9), kind=kCustom, calls=%fused_computation | custom fusion | bytes 4198400 | tf_op jit(solution)/shard_map/jit(_take)/gather | solution.py:33
  19.4 3.8 select_bitcast_fusion
  23.3 53.2 %all_to_all.35 = bf16[2,4,1024,128]{3,1,0,2:T(4,128)(2,1)S(1)} all-to-all(bf16[2,4,1024,128]{3,1,0,2:T(4,128)(2,1)S(1)} %select_bitcast_fusion), channel_id=1, replica_groups=mesh['lat'=4,'wave'=64] {'wave'}, dimensions={2} | all-to-all | bytes 4194304 | tf_op jit(solution)/shard_map/all_to_all | solution.py:34
  76.5 0.6 copy.33
  77.2 1.4 fusion.8
  78.6 2.5 stack.2
  81.0 18.6 %all-to-all-start.1 = ((bf16[4,256,16,128]{3,2,1,0:T(8,128)(2,1)}), bf16[4,256,16,128]{3,2,1,0:T(8,128)(2,1)}, u32[]{:S(2)}, u32[]{:S(2)}) async-start(bf16[4,256,16,128]{3,2,1,0:T(8,128)(2,1)} %stack.2), calls=%async_computation.1 | async-start | bytes 8388608 | tf_op jit(solution)/shard_map/all_to_all | solution.py:9
  99.6 12.6 %copy.20 = bf16[16,256,1024]{1,0,2:T(8,128)(2,1)} copy(bf16[16,256,1024]{2,1,0:T(8,128)(2,1)} %param.7) | data formatting | bytes 16777216 | tf_op args[3]
  112.2 82.1 %all-to-all-done.1 = bf16[4,256,16,128]{3,2,1,0:T(8,128)(2,1)} async-done(((bf16[4,256,16,128]{3,2,1,0:T(8,128)(2,1)}), bf16[4,256,16,128]{3,2,1,0:T(8,128)(2,1)}, u32[]{:S(2)}, u32[]{:S(2)}) %all-to-all-start.1) | async-done | bytes 4194336 | tf_op jit(solution)/shard_map/all_to_all | solution.py:9
  194.3 5.6 %all-to-all-start.2 = ((bf16[16,256,1024]{1,0,2:T(8,128)(2,1)}), bf16[16,256,1024]{1,0,2:T(8,128)(2,1)}, u32[]{:S(2)}, u32[]{:S(2)}) async-start(bf16[16,256,1024]{1,0,2:T(8,128)(2,1)} %copy.20), calls=%async_computation.2 | async-start | bytes 16777216 | tf_op jit(solution)/shard_map/all_to_all | solution.py:39
  199.9 0.0 all-gather.2.cloned.1.call-start
  200.0 0.7 all-gather.2.cloned.1.call-update
  200.7 150.5 %all-gather.2.cloned.1.call-done = bf16[1024,16,128]{2,1,0:T(8,128)(2,1)} async-done(((bf16[256,16,128]{2,1,0:T(8,128)(2,1)}), bf16[1024,16,128]{2,1,0:T(8,128)(2,1)}) %all-gather.2.cloned.1.call-update) | async-done | bytes 4194320 | tf_op jit(solution)/shard_map/all_gather | solution.py:45
  351.2 4.6 bitcast_select_fusion
  355.8 94.3 %all-to-all-done.2 = bf16[16,256,1024]{1,0,2:T(8,128)(2,1)} async-done(((bf16[16,256,1024]{1,0,2:T(8,128)(2,1)}), bf16[16,256,1024]{1,0,2:T(8,128)(2,1)}, u32[]{:S(2)}, u32[]{:S(2)}) %all-to-all-start.2) | async-done | bytes 8388640 | tf_op jit(solution)/shard_map/all_to_all | solution.py:39
  450.1 13.7 %copy.22 = bf16[16,256,4,256]{3,1,0,2:T(8,128)(2,1)} copy(bf16[16,256,4,256]{1,0,3,2:T(8,128)(2,1)} %bitcast.7) | data formatting | bytes 16777216 | tf_op jit(solution)/shard_map/all_to_all | solution.py:39
  463.9 6.3 %convert_reduce_fusion = bf16[16,128,256]{2,1,0:T(8,128)(2,1)S(1)} fusion(bf16[16,256,4,256]{3,1,0,2:T(8,128)(2,1)} %copy.22, bf16[4,256,16,128]{3,2,1,0:T(8,128)(2,1)} %bitcast.20), kind=kOutput, calls=%fused_computation.5 | convolution fusion | flops 1077411840 | bytes 13631488 | tf_op jit(solution)/shard_map/mbkl,bkmc->bmlc/dot_general | solution.py:19
  470.2 1.3 copy.24
  (1 shorter events, 0.0 us)
Async XLA Ops:
  81.0 113.3 %all-to-all-start.1 = ((bf16[4,256,16,128]{3,2,1,0:T(8,128)(2,1)}), bf16[4,256,16,128]{3,2,1,0:T(8,128)(2,1)}, u32[]{:S(2)}, u32[]{:S(2)}) async-start(bf16[4,256,16,128]{3,2,1,0:T(8,128)(2,1)} %stack.2), calls=%async_computation.1 | async-start | bytes 8388608 | tf_op jit(solution)/shard_map/all_to_all | solution.py:9
  194.3 255.8 %all-to-all-start.2 = ((bf16[16,256,1024]{1,0,2:T(8,128)(2,1)}), bf16[16,256,1024]{1,0,2:T(8,128)(2,1)}, u32[]{:S(2)}, u32[]{:S(2)}) async-start(bf16[16,256,1024]{1,0,2:T(8,128)(2,1)} %copy.20), calls=%async_computation.2 | async-start | bytes 16777216 | tf_op jit(solution)/shard_map/all_to_all | solution.py:39
  199.9 151.3 %all-gather.2.cloned.1.call-start = ((), (), s32[]{:S(2)}) async-start(), calls=%async_computation.3 | async-start | bytes 5242880 | tf_op jit(solution)/shard_map/all_gather | solution.py:45
Sparse Core Ops, SparseCore 0:
  202.6 148.5 all-gather.1
